TPU v7x, 128 devices: a whole 4x4x4 slice. The times are simulated.
128 devices in a mesh: src: 8 (over y, core), rcv: 16 (over x, z).
Axes of the slice: x: 4, y: 4, z: 4, core: 2. Of those that a mesh axis runs over, the one named last changes fastest.
Arguments:
- recorded: float32 [1024, 1024, 512], P('src', 'rcv'), may hold values from -16 to 16, as said below
- owner_map: int32 [64], replicated, may hold values from 0 to 127, as said below
Outputs:
- squares: bfloat16 [128, 2, 2, 1024, 1024], P(('src', 'rcv'))
Inputs may be any that keep to these rules, and one draw needn't show every extreme that they name: `recorded`: every trace is noise times a trace amplitude of its own. `owner_map`: no device owns more than 2 frequencies, and some device owns exactly 2.
All inputs are finite; a program needn't handle non-finite values.
Results may differ from a plain program's by a relative error of at most 0.0076.
Values may be sent and summed in bfloat16 or wider, within the bound.
A program may use at most 192 MiB of HBM per device.

v0:
```python
import functools
import math

import jax
import jax.numpy as jnp
import numpy as np
from jax import lax
from jax.experimental import pallas as pl
from jax.experimental.pallas import tpu as pltpu
from jax.sharding import PartitionSpec as P

FIRST = 4
CAP = 2
WATER = 0.5
NT = 512
NF = 64
N = 1024
NDEV = 128
TILES = NDEV + 8
CHUNK = 16
STEPS = 64 // CHUNK
VMEM_LIMIT = 62 * 1024 * 1024
MESH = pl.DeviceIdType.MESH


def basis_parts():
    t = np.arange(NT)[:, None]
    f = np.arange(NF)[None, :] + FIRST
    angles = 2.0 * math.pi * ((t * f) % NT) / NT
    both = np.concatenate([np.cos(angles), -np.sin(angles)], axis=1) / math.sqrt(NT)
    high = both.astype(jnp.bfloat16)
    low = (both - high.astype(np.float64)).astype(jnp.bfloat16)
    return np.concatenate([high, low], axis=1)


def merge(own, mirror):
    def power(v):
        square = v * v
        return square + pltpu.roll(square, 64, axis=square.ndim - 1)

    p_own, p_mirror = power(own), power(mirror)
    inv = 1.0 / (p_own + p_mirror + WATER)
    return ((p_own + 0.5 * WATER) * own + (p_mirror + 0.5 * WATER) * mirror) * inv


def peer(k, x, y, z, c):
    dx = k % 4
    dy = (k // 4 + dx) % 4
    dz = (k // 16 + dy) % 4
    xs, ys, zs, cs = (x + dx) % 4, (y + dy) % 4, (z + dz) % 4, (c + k // 64) % 2
    return ys * 2 + cs, xs * 4 + zs


def exchange_kernel(
    table, x_hbm, basis_ref, got0, got1,
    xa, xb, wide, turned, kept, sent, mirror, select, extra,
    load_a, load_b, send_m, recv_m, send_o, recv_o, send_e, own_sem,
):
    i, q = lax.axis_index("src"), lax.axis_index("rcv")
    y, c = i // 2, i % 2
    x, z = q // 4, q % 4
    me = i * 16 + q
    first = q == 2 * i
    second = q == 2 * i + 1
    keep = jnp.where(q > 2 * i + 1, 1 - q % 2, jnp.where(q < 2 * i, q % 2, 0))
    away = 1 - keep
    got = (got0, got1)

    barrier = pltpu.get_barrier_semaphore()

    @pl.loop(1, NDEV)
    def _(k):
        pl.semaphore_signal(barrier, inc=1, device_id=peer(k, x, y, z, c), device_id_type=MESH)

    def fetch_a(k):
        src = x_hbm.at[pl.ds(64 * away + CHUNK * k, CHUNK)]
        return pltpu.make_async_copy(src, xa.at[k % 2], load_a.at[k % 2])

    def fetch_b(k):
        src = x_hbm.at[pl.ds(64 * keep, 64), pl.ds(CHUNK * k, CHUNK)]
        return pltpu.make_async_copy(src, xb.at[k % 2], load_b.at[k % 2])

    for k in range(2):
        fetch_a(k).start()
    for k in range(2):
        fetch_b(k).start()

    ch = 2 * NF

    def transform(values):
        high = values.astype(jnp.bfloat16)
        low = (values - high.astype(jnp.float32)).astype(jnp.bfloat16)
        one = jnp.dot(high, basis_ref[...], preferred_element_type=jnp.float32)
        two = jnp.dot(low, basis_ref[:, :ch], preferred_element_type=jnp.float32)
        wide[...] = one[:, :ch] + one[:, ch:] + two

    def turn(rows_of, k, out):
        low_half = lax.broadcasted_iota(jnp.int32, (NF, 128), 1) < 64
        for j in range(CHUNK // 2):
            both = rows_of(j).T
            real, imag = both[:NF], both[NF:]
            turned[pl.ds(2 * j, NF, stride=CHUNK), :] = jnp.where(low_half, real, pltpu.roll(imag, 64, axis=1))
            turned[pl.ds(2 * j + 1, NF, stride=CHUNK), :] = jnp.where(low_half, pltpu.roll(real, 64, axis=1), imag)
        rows = pl.ds(pl.multiple_of(k * CHUNK, CHUNK), CHUNK)
        out[:, rows, :] = turned[...].reshape(NF, CHUNK, 128).astype(jnp.bfloat16)

    def mirror_copy(k):
        rows = pl.ds(pl.multiple_of(k * CHUNK, CHUNK), CHUNK)
        return pltpu.make_async_remote_copy(
            src_ref=sent.at[:, rows, :],
            dst_ref=mirror.at[:, rows, :],
            send_sem=send_m.at[k],
            recv_sem=recv_m.at[k],
            device_id=(q // 2, 2 * i + away),
            device_id_type=MESH,
        )

    @pl.loop(0, STEPS)
    def _(k):
        fetch_a(k).wait()
        transform(xa[k % 2].reshape(CHUNK * 64, NT))

        @pl.when(k + 2 < STEPS)
        def _():
            fetch_a(k + 2).start()

        turn(lambda j: wide[pl.ds(128 * j, 128), :], k, sent)

        @pl.when(k == 0)
        def _():
            pl.semaphore_wait(barrier, NDEV - 1)

        @pl.when(jnp.logical_not(second))
        def _():
            mirror_copy(k).start()

    def strided(j):
        parts = [wide[pl.ds(2 * j + h, 64, stride=CHUNK), :] for h in range(2)]
        return jnp.concatenate(parts, axis=0)

    @pl.loop(0, STEPS)
    def _(k):
        fetch_b(k).wait()
        transform(xb[k % 2].reshape(CHUNK * 64, NT))

        @pl.when(k + 2 < STEPS)
        def _():
            fetch_b(k + 2).start()

        turn(strided, k, kept)

    @pl.when(jnp.logical_not(first))
    def _():
        @pl.loop(0, STEPS)
        def _(k):
            mirror_copy(k).wait_recv()
            rows = pl.ds(pl.multiple_of(k * CHUNK, CHUNK), CHUNK)

            @pl.loop(0, NF // 4)
            def _(f):
                own = kept[pl.ds(f * 4, 4), rows, :].astype(jnp.float32)
                other = mirror[pl.ds(f * 4, 4), rows, :].astype(jnp.float32)
                kept[pl.ds(f * 4, 4), rows, :] = merge(own, other).astype(jnp.bfloat16)

    def extra_copy(slot, k):
        device = peer(k, x, y, z, c)
        return pltpu.make_async_remote_copy(
            src_ref=extra.at[slot, device[0] * 16 + device[1]],
            dst_ref=got[slot].at[NDEV + i],
            send_sem=send_e.at[slot],
            recv_sem=recv_o.at[slot],
            device_id=device,
            device_id_type=MESH,
        )

    def owner_copy(slot, k):
        device = peer(k, x, y, z, c)
        return pltpu.make_async_remote_copy(
            src_ref=select.at[slot, device[0] * 16 + device[1]],
            dst_ref=got[slot].at[me],
            send_sem=send_o.at[slot],
            recv_sem=recv_o.at[slot],
            device_id=device,
            device_id_type=MESH,
        )

    def local_copies(slot):
        own = pltpu.make_async_copy(select.at[slot, me], got[slot].at[me], own_sem.at[slot])
        more = pltpu.make_async_copy(extra.at[slot, me], got[slot].at[NDEV + i], own_sem.at[2 + slot])
        return own, more

    for slot in range(CAP):
        @pl.loop(0, NDEV)
        def _(d):
            select[slot, d] = kept[table[slot, d]]

        @pl.when(second)
        def _():
            @pl.loop(0, NDEV)
            def _(d):
                extra[slot, d] = sent[table[slot, d]]

    for slot in range(CAP):
        own, more = local_copies(slot)
        own.start()

        @pl.when(jnp.logical_not(second))
        def _():
            @pl.loop(1, NDEV)
            def _(k):
                owner_copy(slot, k).start()

        @pl.when(second)
        def _():
            more.start()

            @pl.loop(1, NDEV)
            def _(k):
                owner_copy(slot, k).start()
                extra_copy(slot, k).start()

    @pl.when(jnp.logical_not(second))
    def _():
        @pl.loop(0, STEPS)
        def _(k):
            mirror_copy(k).wait_send()

    for slot in range(CAP):
        own, more = local_copies(slot)
        own.wait()
        most = select.at[slot, pl.ds(0, NDEV - 1)]
        pltpu.make_async_copy(most, most, send_o.at[slot]).wait()

        def arrived(count):
            part = got[slot].at[pl.ds(0, count)]
            pltpu.make_async_copy(part, part, recv_o.at[slot]).wait()

        @pl.when(second)
        def _():
            more.wait()
            pltpu.make_async_copy(most, most, send_e.at[slot]).wait()
            arrived(TILES - 2)

        @pl.when(jnp.logical_not(second))
        def _():
            arrived(TILES - 1)


def tiles_at_owners(recorded, table):
    tile = (64, 128)
    dma = pltpu.SemaphoreType.DMA
    return pl.pallas_call(
        exchange_kernel,
        out_shape=[jax.ShapeDtypeStruct((TILES,) + tile, jnp.bfloat16)] * 2,
        in_specs=[
            pl.BlockSpec(memory_space=pltpu.SMEM),
            pl.BlockSpec(memory_space=pl.ANY),
            pl.BlockSpec(memory_space=pltpu.VMEM),
        ],
        out_specs=[pl.BlockSpec(memory_space=pl.ANY)] * 2,
        scratch_shapes=[
            pltpu.VMEM((2, CHUNK, 64, NT), jnp.float32),
            pltpu.VMEM((2, 64, CHUNK, NT), jnp.float32),
            pltpu.VMEM((CHUNK * 64, 2 * NF), jnp.float32),
            pltpu.VMEM((NF * CHUNK, 128), jnp.float32),
            pltpu.VMEM((NF,) + tile, jnp.bfloat16),
            pltpu.VMEM((NF,) + tile, jnp.bfloat16),
            pltpu.VMEM((NF,) + tile, jnp.bfloat16),
            pltpu.VMEM((CAP, NDEV) + tile, jnp.bfloat16),
            pltpu.VMEM((CAP, NDEV) + tile, jnp.bfloat16),
            dma((2,)), dma((2,)), dma((STEPS,)), dma((STEPS,)),
            dma((CAP,)), dma((CAP,)), dma((CAP,)), dma((2 * CAP,)),
        ],
        compiler_params=pltpu.CompilerParams(
            vmem_limit_bytes=VMEM_LIMIT, collective_id=0, has_side_effects=True
        ),
        name="exchange",
    )(table, recorded, jnp.asarray(basis_parts()))


def square_kernel(owned_ref, got0, got1, out, got, mat, res, sem_in, sems):
    for slot in range(CAP):
        @pl.when(owned_ref[slot] != 0)
        def _():
            pltpu.make_async_copy((got0, got1)[slot], got.at[slot], sem_in.at[slot]).start()

    def copy_out(slot, row, col):
        r = pl.multiple_of(row * 256, 256)
        c = pl.multiple_of(col * 256, 256)
        return pltpu.make_async_copy(
            res.at[slot, :, pl.ds(r, 256), pl.ds(c, 256)],
            out.at[0, slot, :, pl.ds(r, 256), pl.ds(c, 256)],
            sems.at[slot * 16 + row * 4 + col],
        )

    low = lax.broadcasted_iota(jnp.int32, (64, 128), 1) < 64

    def swap(v):
        return pltpu.roll(v, 64, axis=1)

    def put(a, b, top, bottom):
        ra = pl.multiple_of(a * 128, 128)
        rb = pl.multiple_of(b * 128, 128)
        for c in range(2):
            block = jnp.concatenate([top[c], bottom[c]], axis=0)
            mat[c, pl.ds(ra, 128), pl.ds(rb, 128)] = block.astype(jnp.bfloat16)
            mat[c, pl.ds(rb, 128), pl.ds(ra, 128)] = block.T.astype(jnp.bfloat16)

    @pl.loop(0, CAP)
    def _(slot):
        @pl.when(owned_ref[slot] == 0)
        def _():
            res[slot] = jnp.zeros((2, N, N), jnp.bfloat16)

            @pl.loop(0, 4)
            def _(row):
                @pl.loop(0, 4)
                def _(col):
                    copy_out(slot, row, col).start()

        @pl.when(owned_ref[slot] != 0)
        def _():
            pltpu.make_async_copy(got0, got.at[slot], sem_in.at[slot]).wait()

            def tile(k):
                return got[slot, k].astype(jnp.float32)

            @pl.loop(0, 8)
            def _(b):
                @pl.loop(0, b)
                def _(a):
                    t00, t11 = tile(b * 16 + 2 * a), tile(b * 16 + 2 * a + 1)
                    u01, u10 = tile(a * 16 + 2 * b + 1), tile(a * 16 + 2 * b)
                    both = jnp.concatenate([u01, u10], axis=0).T
                    real, imag = swap(both[:64]), swap(both[64:])
                    top = (jnp.where(low, t00, real), jnp.where(low, swap(t00), imag))
                    bottom = (jnp.where(low, real, swap(t11)), jnp.where(low, imag, t11))
                    put(a, b, top, bottom)

                d0, d1, u = tile(b * 16 + 2 * b), tile(NDEV + b), tile(b * 16 + 2 * b + 1)
                both = jnp.concatenate([d0, d1], axis=0).T
                d0 = merge(d0, jnp.where(low, both[:64], swap(both[64:])))
                d1 = merge(d1, jnp.where(low, swap(both[:64]), both[64:]))
                other = jnp.concatenate([u, u], axis=0).T
                top = (jnp.where(low, d0, other[:64]), jnp.where(low, swap(d0), other[64:]))
                bottom = (jnp.where(low, u, swap(d1)), jnp.where(low, swap(u), d1))
                put(b, b, top, bottom)

            @pl.loop(0, 4)
            def _(col):
                cc = pl.multiple_of(col * 256, 256)

                @pl.loop(0, col + 1)
                def _(row):
                    rr = pl.multiple_of(row * 256, 256)

                    def dot(left, right):
                        return jnp.dot(
                            mat[left, pl.ds(rr, 256), :],
                            mat[right, :, pl.ds(cc, 256)],
                            preferred_element_type=jnp.float32,
                        )

                    factor = 1.0 / math.sqrt(N)
                    real = (dot(0, 0) - dot(1, 1)) * factor
                    imag = (dot(0, 1) + dot(1, 0)) * factor
                    for c, part in enumerate((real, imag)):
                        res[slot, c, pl.ds(rr, 256), pl.ds(cc, 256)] = part.astype(jnp.bfloat16)
                        res[slot, c, pl.ds(cc, 256), pl.ds(rr, 256)] = part.T.astype(jnp.bfloat16)
                    copy_out(slot, row, col).start()

                    @pl.when(row != col)
                    def _():
                        copy_out(slot, col, row).start()

    @pl.loop(0, CAP)
    def _(slot):
        @pl.loop(0, 4)
        def _(row):
            @pl.loop(0, 4)
            def _(col):
                copy_out(slot, row, col).wait()


def squares_of(owned, got0, got1):
    return pl.pallas_call(
        square_kernel,
        out_shape=jax.ShapeDtypeStruct((1, CAP, 2, N, N), jnp.bfloat16),
        in_specs=[pl.BlockSpec(memory_space=pltpu.SMEM)] + [pl.BlockSpec(memory_space=pl.ANY)] * 2,
        out_specs=pl.BlockSpec(memory_space=pl.ANY),
        scratch_shapes=[
            pltpu.VMEM((CAP, TILES, 64, 128), jnp.bfloat16),
            pltpu.VMEM((2, N, N), jnp.bfloat16),
            pltpu.VMEM((CAP, 2, N, N), jnp.bfloat16),
            pltpu.SemaphoreType.DMA((CAP,)),
            pltpu.SemaphoreType.DMA((CAP * 16,)),
        ],
        compiler_params=pltpu.CompilerParams(vmem_limit_bytes=VMEM_LIMIT),
        name="squares",
    )(owned, got0, got1)


def shards(recorded, owner_map):
    bands = jnp.arange(NF, dtype=jnp.int32)
    shared = owner_map[:, None] == owner_map[None, :]
    slot_of = jnp.sum((shared & (bands[None, :] < bands[:, None])).astype(jnp.int32), axis=1)
    places = jnp.arange(CAP * NDEV, dtype=jnp.int32).reshape(CAP, NDEV)
    hit = (slot_of * NDEV + owner_map)[None, None, :] == places[:, :, None]
    table = jnp.sum(jnp.where(hit, bands[None, None, :], 0), axis=2)
    me = lax.axis_index("src") * lax.axis_size("rcv") + lax.axis_index("rcv")
    mine = jnp.sum((owner_map == me).astype(jnp.int32))
    owned = (mine > jnp.arange(CAP, dtype=jnp.int32)).astype(jnp.int32)
    got0, got1 = tiles_at_owners(recorded, table)
    return squares_of(owned, got0, got1)


def solution(mesh):
    in_specs = (P("src", "rcv", None), P())
    out_specs = P(("src", "rcv"), None, None, None, None)
    return jax.shard_map(shards, mesh=mesh, in_specs=in_specs, out_specs=out_specs, check_vma=False)
```

profile of v0, /device:TPU:7, one launch (start us, length us, event | category | flops | bytes accessed | tf_op | source)
XLA Modules:
  0.0 159.8 jit_solution(16833468057473197049)
XLA Ops:
  0.0 0.9 convert_reduce_fusion
  0.9 1.3 multiply_add_fusion.1
  2.2 1.2 compare_convert_fusion.owned_ref
  3.4 0.7 select_reduce_fusion.table
  4.0 113.2 %exchange.1 = (bf16[136,64,128]{2,1,0:T(8,128)(2,1)}, bf16[136,64,128]{2,1,0:T(8,128)(2,1)}) custom-call(s32[2,128]{1,0:T(2,128)} %select_reduce_fusion.table, f32[128,64,512]{2,1,0:T(8,128)} %x_hbm.1, bf16[512,256]{1,0:T(8,128)(2,1)} %constant.18.clone.basis_ref), custom_call_target="tpu_custom_call" | custom-call | tf_op jit(solution)/shard_map/exchange/pallas_call | solution.py:252
  117.2 42.5 %squares.1 = bf16[1,2,2,1024,1024]{4,3,2,1,0:T(8,128)(2,1)} custom-call(s32[2]{0:T(128)} %compare_convert_fusion.owned_ref, bf16[136,64,128]{2,1,0:T(8,128)(2,1)} %get-tuple-element.7.got0, bf16[136,64,128]{2,1,0:T(8,128)(2,1)} %get-tuple-element.8.got1), custom_call_target="tpu_custom_call" | custom-call | tf_op jit(solution)/shard_map/squares/pallas_call | solution.py:386
  (1 shorter events, 0.0 us)
where the time goes:
time: 162 us; the launch traced here: 160 us
  Pallas kernels  156 us (96%)
  other arithmetic  4.03 us (2%)
    pallas_call x1, Pallas kernels, tiles_at_owners(): pl.pallas_call(exchange_kernel, out_shape=[jax.ShapeDtypeStruct((TILES,)...  113 us
    pallas_call x1, Pallas kernels, squares_of(): pl.pallas_call(square_kernel, out_shape=jax.ShapeDtypeStruct((1, CAP, 2,...  42.5 us

commit v1 on v0

--- a/solution.py
+++ b/solution.py
@@ -51,10 +51,14 @@
     return ys * 2 + cs, xs * 4 + zs
 
 
+def away_half(i, q):
+    return jnp.where(q > 2 * i + 1, q % 2, jnp.where(q < 2 * i, 1 - q % 2, 1))
+
+
 def exchange_kernel(
     table, x_hbm, basis_ref, got0, got1,
-    xa, xb, wide, turned, kept, sent, mirror, select, extra,
-    load_a, load_b, send_m, recv_m, send_o, recv_o, send_e, own_sem,
+    xa, xb, wide, turned, kept, sent, mirror, relay, select, extra,
+    load_a, load_b, send_m, recv_m, send_r, recv_r, send_o, recv_o, send_e, own_sem,
 ):
     i, q = lax.axis_index("src"), lax.axis_index("rcv")
     y, c = i // 2, i % 2
@@ -62,8 +66,9 @@
     me = i * 16 + q
     first = q == 2 * i
     second = q == 2 * i + 1
-    keep = jnp.where(q > 2 * i + 1, 1 - q % 2, jnp.where(q < 2 * i, q % 2, 0))
-    away = 1 - keep
+    far = (x + 2) % 4 == y
+    away = away_half(i, q)
+    keep = 1 - away
     got = (got0, got1)
 
     barrier = pltpu.get_barrier_semaphore()
@@ -115,6 +120,35 @@
             device_id_type=MESH,
         )
 
+    def chunk_of(ref, k):
+        return ref.at[:, pl.ds(pl.multiple_of(k * CHUNK, CHUNK), CHUNK), :]
+
+    def relay_in(k):
+        step = 1 + 2 * (k % 2)
+        xs, ys = (x + step) % 4, (y + step) % 4
+        return pltpu.make_async_remote_copy(
+            src_ref=chunk_of(sent, k),
+            dst_ref=relay.at[k],
+            send_sem=send_m.at[k],
+            recv_sem=recv_r.at[k],
+            device_id=(ys * 2 + c, xs * 4 + z),
+            device_id_type=MESH,
+        )
+
+    def relay_out(k):
+        step = 3 - 2 * (k % 2)
+        i_from, q_from = ((y + step) % 4) * 2 + c, ((x + step) % 4) * 4 + z
+        return pltpu.make_async_remote_copy(
+            src_ref=relay.at[k],
+            dst_ref=chunk_of(mirror, k),
+            send_sem=send_r.at[k],
+            recv_sem=recv_m.at[k],
+            device_id=(q_from // 2, 2 * i_from + away_half(i_from, q_from)),
+            device_id_type=MESH,
+        )
+
+    near = jnp.logical_not(jnp.logical_or(second, far))
+
     @pl.loop(0, STEPS)
     def _(k):
         fetch_a(k).wait()
@@ -130,9 +164,13 @@
         def _():
             pl.semaphore_wait(barrier, NDEV - 1)
 
-        @pl.when(jnp.logical_not(second))
+        @pl.when(near)
         def _():
             mirror_copy(k).start()
+
+        @pl.when(far)
+        def _():
+            relay_in(k).start()
 
     def strided(j):
         parts = [wide[pl.ds(2 * j + h, 64, stride=CHUNK), :] for h in range(2)]
@@ -148,6 +186,11 @@
             fetch_b(k + 2).start()
 
         turn(strided, k, kept)
+
+        @pl.when(far)
+        def _():
+            relay_in(k).wait_recv()
+            relay_out(k).start()
 
     @pl.when(jnp.logical_not(first))
     def _():
@@ -219,11 +262,18 @@
                 owner_copy(slot, k).start()
                 extra_copy(slot, k).start()
 
-    @pl.when(jnp.logical_not(second))
+    @pl.when(near)
     def _():
         @pl.loop(0, STEPS)
         def _(k):
             mirror_copy(k).wait_send()
+
+    @pl.when(far)
+    def _():
+        @pl.loop(0, STEPS)
+        def _(k):
+            relay_in(k).wait_send()
+            relay_out(k).wait_send()
 
     for slot in range(CAP):
         own, more = local_copies(slot)
@@ -266,9 +316,10 @@
             pltpu.VMEM((NF,) + tile, jnp.bfloat16),
             pltpu.VMEM((NF,) + tile, jnp.bfloat16),
             pltpu.VMEM((NF,) + tile, jnp.bfloat16),
+            pltpu.VMEM((STEPS, NF, CHUNK, 128), jnp.bfloat16),
             pltpu.VMEM((CAP, NDEV) + tile, jnp.bfloat16),
             pltpu.VMEM((CAP, NDEV) + tile, jnp.bfloat16),
-            dma((2,)), dma((2,)), dma((STEPS,)), dma((STEPS,)),
+            dma((2,)), dma((2,)), dma((STEPS,)), dma((STEPS,)), dma((STEPS,)), dma((STEPS,)),
             dma((CAP,)), dma((CAP,)), dma((CAP,)), dma((2 * CAP,)),
         ],
         compiler_params=pltpu.CompilerParams(
@@ -278,7 +329,12 @@
     )(table, recorded, jnp.asarray(basis_parts()))
 
 
-def square_kernel(owned_ref, got0, got1, out, got, mat, res, sem_in, sems):
+def square_kernel(owner_ref, got0, got1, out, owned_ref, got, mat, res, sem_in, sems):
+    me = lax.axis_index("src") * 16 + lax.axis_index("rcv")
+    mine = lax.fori_loop(0, NF, lambda f, n: n + jnp.where(owner_ref[f] == me, 1, 0), 0)
+    for slot in range(CAP):
+        owned_ref[slot] = jnp.where(mine > slot, 1, 0)
+
     for slot in range(CAP):
         @pl.when(owned_ref[slot] != 0)
         def _():
@@ -302,9 +358,8 @@
         ra = pl.multiple_of(a * 128, 128)
         rb = pl.multiple_of(b * 128, 128)
         for c in range(2):
-            block = jnp.concatenate([top[c], bottom[c]], axis=0)
-            mat[c, pl.ds(ra, 128), pl.ds(rb, 128)] = block.astype(jnp.bfloat16)
-            mat[c, pl.ds(rb, 128), pl.ds(ra, 128)] = block.T.astype(jnp.bfloat16)
+            mat[c, pl.ds(ra, 64), pl.ds(rb, 128)] = top[c].astype(jnp.bfloat16)
+            mat[c, pl.ds(ra + 64, 64), pl.ds(rb, 128)] = bottom[c].astype(jnp.bfloat16)
 
     @pl.loop(0, CAP)
     def _(slot):
@@ -325,18 +380,21 @@
             def tile(k):
                 return got[slot, k].astype(jnp.float32)
 
-            @pl.loop(0, 8)
-            def _(b):
-                @pl.loop(0, b)
-                def _(a):
-                    t00, t11 = tile(b * 16 + 2 * a), tile(b * 16 + 2 * a + 1)
-                    u01, u10 = tile(a * 16 + 2 * b + 1), tile(a * 16 + 2 * b)
-                    both = jnp.concatenate([u01, u10], axis=0).T
-                    real, imag = swap(both[:64]), swap(both[64:])
-                    top = (jnp.where(low, t00, real), jnp.where(low, swap(t00), imag))
-                    bottom = (jnp.where(low, real, swap(t11)), jnp.where(low, imag, t11))
-                    put(a, b, top, bottom)
-
+            def pair(a, b):
+                t00, t11 = tile(b * 16 + 2 * a), tile(b * 16 + 2 * a + 1)
+                u01, u10 = tile(a * 16 + 2 * b + 1), tile(a * 16 + 2 * b)
+                turned = jnp.concatenate([u01, u10], axis=0).T
+                real, imag = swap(turned[:64]), swap(turned[64:])
+                top = (jnp.where(low, t00, real), jnp.where(low, swap(t00), imag))
+                bottom = (jnp.where(low, real, swap(t11)), jnp.where(low, imag, t11))
+                put(a, b, top, bottom)
+                turned = jnp.concatenate([t00, t11], axis=0).T
+                real, imag = turned[:64], turned[64:]
+                top = (jnp.where(low, real, swap(u10)), jnp.where(low, imag, u10))
+                bottom = (jnp.where(low, u01, real), jnp.where(low, swap(u01), imag))
+                put(b, a, top, bottom)
+
+            def diagonal(b):
                 d0, d1, u = tile(b * 16 + 2 * b), tile(NDEV + b), tile(b * 16 + 2 * b + 1)
                 both = jnp.concatenate([d0, d1], axis=0).T
                 d0 = merge(d0, jnp.where(low, both[:64], swap(both[64:])))
@@ -346,6 +404,18 @@
                 bottom = (jnp.where(low, u, swap(d1)), jnp.where(low, swap(u), d1))
                 put(b, b, top, bottom)
 
+            @pl.loop(0, 7)
+            def _(k):
+                pair(k, 7)
+                for j in range(1, 4):
+                    one, two = (k + j) % 7, (k + 7 - j) % 7
+                    pair(jnp.minimum(one, two), jnp.maximum(one, two))
+
+            @pl.loop(0, 4)
+            def _(b):
+                diagonal(2 * b)
+                diagonal(2 * b + 1)
+
             @pl.loop(0, 4)
             def _(col):
                 cc = pl.multiple_of(col * 256, 256)
@@ -382,13 +452,14 @@
                 copy_out(slot, row, col).wait()
 
 
-def squares_of(owned, got0, got1):
+def squares_of(owner_map, got0, got1):
     return pl.pallas_call(
         square_kernel,
         out_shape=jax.ShapeDtypeStruct((1, CAP, 2, N, N), jnp.bfloat16),
         in_specs=[pl.BlockSpec(memory_space=pltpu.SMEM)] + [pl.BlockSpec(memory_space=pl.ANY)] * 2,
         out_specs=pl.BlockSpec(memory_space=pl.ANY),
         scratch_shapes=[
+            pltpu.SMEM((CAP,), jnp.int32),
             pltpu.VMEM((CAP, TILES, 64, 128), jnp.bfloat16),
             pltpu.VMEM((2, N, N), jnp.bfloat16),
             pltpu.VMEM((CAP, 2, N, N), jnp.bfloat16),
@@ -397,21 +468,17 @@
         ],
         compiler_params=pltpu.CompilerParams(vmem_limit_bytes=VMEM_LIMIT),
         name="squares",
-    )(owned, got0, got1)
+    )(owner_map, got0, got1)
 
 
 def shards(recorded, owner_map):
-    bands = jnp.arange(NF, dtype=jnp.int32)
-    shared = owner_map[:, None] == owner_map[None, :]
-    slot_of = jnp.sum((shared & (bands[None, :] < bands[:, None])).astype(jnp.int32), axis=1)
-    places = jnp.arange(CAP * NDEV, dtype=jnp.int32).reshape(CAP, NDEV)
-    hit = (slot_of * NDEV + owner_map)[None, None, :] == places[:, :, None]
-    table = jnp.sum(jnp.where(hit, bands[None, None, :], 0), axis=2)
-    me = lax.axis_index("src") * lax.axis_size("rcv") + lax.axis_index("rcv")
-    mine = jnp.sum((owner_map == me).astype(jnp.int32))
-    owned = (mine > jnp.arange(CAP, dtype=jnp.int32)).astype(jnp.int32)
+    bands = jnp.arange(NF, dtype=jnp.int32)[None, :]
+    hit = owner_map[None, :] == jnp.arange(NDEV, dtype=jnp.int32)[:, None]
+    lowest = jnp.min(jnp.where(hit, bands, NF - 1), axis=1)
+    highest = jnp.max(jnp.where(hit, bands, 0), axis=1)
+    table = jnp.stack([lowest, highest])
     got0, got1 = tiles_at_owners(recorded, table)
-    return squares_of(owned, got0, got1)
+    return squares_of(owner_map, got0, got1)
 
 
 def solution(mesh):

time: 162 us -> 133 us (0.82)
  the two profiles are of different devices: /device:TPU:7 before, /device:TPU:108 now
where the time goes in v1:
time: 133 us; the launch traced here: 131 us
  Pallas kernels  130 us (98%)
    pallas_call x1, Pallas kernels, tiles_at_owners(): pl.pallas_call(exchange_kernel, out_shape=[jax.ShapeDtypeStruct((TILES,)...  99.6 us
    pallas_call x1, Pallas kernels, squares_of(): pl.pallas_call(square_kernel, out_shape=jax.ShapeDtypeStruct((1, CAP, 2,...  30.2 us

profile of v1, /device:TPU:108, one launch (start us, length us, event | category | flops | bytes accessed | tf_op | source)
XLA Modules:
  0.0 131.1 jit_solution(9698332631249942645)
XLA Ops:
  0.0 0.7 select_reduce_fusion.1
  0.7 0.6 pad_add_fusion.table
  1.3 99.6 %exchange.1 = (bf16[136,64,128]{2,1,0:T(8,128)(2,1)}, bf16[136,64,128]{2,1,0:T(8,128)(2,1)}) custom-call(s32[2,128]{1,0:T(2,128)} %pad_add_fusion.table, f32[128,64,512]{2,1,0:T(8,128)} %x_hbm.1, bf16[512,256]{1,0:T(8,128)(2,1)} %constant.10.clone.basis_ref), custom_call_target="tpu_custom_call" | custom-call | tf_op jit(solution)/shard_map/exchange/pallas_call | solution.py:302
  100.9 30.2 %squares.1 = bf16[1,2,2,1024,1024]{4,3,2,1,0:T(8,128)(2,1)} custom-call(s32[64]{0:T(128)} %owner_ref.1, bf16[136,64,128]{2,1,0:T(8,128)(2,1)} %get-tuple-element.7.got0, bf16[136,64,128]{2,1,0:T(8,128)(2,1)} %get-tuple-element.8.got1), custom_call_target="tpu_custom_call" | custom-call | tf_op jit(solution)/shard_map/squares/pallas_call | solution.py:456
